TPU v7x, 32 devices: a whole 2x2x4 slice. The times are simulated.
32 devices in a mesh: dp: 8 (over z, y), sub: 4 (over x, core).
Axes of the slice: x: 2, y: 2, z: 4, core: 2. Of those that a mesh axis runs over, the one named last changes fastest.
Arguments:
- queries: bfloat16 [32, 64, 576], P('dp'), may hold values from -195 to 195
- own_cache: bfloat16 [32, 1024, 576], P('dp', 'sub'), may hold values from -8 to 8
- own_len: int32 [32, 4], P('dp', 'sub'), may hold values from 2 to 256
- host_cache: bfloat16 [8, 4, 8, 1024, 576], P('dp', 'sub'), may hold values from -8 to 8
- host_len: int32 [8, 4, 8], P('dp', 'sub'), may hold values from 2 to 1024
- page_plan: int32 [8, 4, 8], P('dp', 'sub'), may hold values from 0 to 3
- value_up: bfloat16 [64, 512, 128], P('sub'), may hold values from -0.25 to 0.25
Outputs:
- attended: bfloat16 [32, 64, 128], P('dp', 'sub')
All inputs are finite; a program needn't handle non-finite values.
Results may differ from a plain program's by a relative error of at most 0.008.
Values may be sent and summed in bfloat16 or wider, within the bound.
No kernel may reach another device: no remote copies, remote signals or barrier semaphores. Data moves between devices by JAX's collectives and lax.ppermute only.
A program may use at most 128 MiB of HBM per device.

v0:
```python
import jax
import jax.numpy as jnp
from jax import lax
from jax.sharding import PartitionSpec as P

DL = 512
score_scale = 192 ** (-0.5)
masked_score = -1e30


def attend(queries, slot_cache, lengths):
    scores = (
        jnp.einsum("phd,ptd->pht", queries, slot_cache, preferred_element_type=jnp.float32)
        * score_scale
    )
    position = lax.broadcasted_iota(jnp.int32, (1, 1, slot_cache.shape[1]), 2)
    scores = jnp.where(position < lengths[:, None, None], scores, masked_score)
    largest = jnp.max(scores, axis=2, keepdims=True)
    exponent = jnp.exp(scores - largest)
    totals = jnp.sum(exponent, axis=2)
    weights = exponent.astype(jnp.bfloat16)
    weighted = jnp.einsum(
        "pht,ptd->phd", weights, slot_cache[:, :, :DL], preferred_element_type=jnp.float32
    )
    return (weighted / totals[:, :, None], largest[:, :, 0] + jnp.log(totals))


def combine_group(device_out, device_lse):
    pieces_out, pieces_lse = (
        lax.all_to_all(device_out[None], "sub", split_axis=2, concat_axis=0, tiled=True),
        lax.all_to_all(device_lse[None], "sub", split_axis=2, concat_axis=0, tiled=True),
    )
    piece_peak = jnp.max(pieces_lse, axis=0)
    piece_weight = jnp.exp(pieces_lse - piece_peak[None])
    weight_total = jnp.sum(piece_weight, axis=0)
    share_out = jnp.sum(piece_weight[..., None] * pieces_out, axis=0) / weight_total[..., None]
    share_lse = piece_peak + jnp.log(weight_total)
    return (share_out, share_lse)


def local(queries, own_cache, own_len, host_cache, host_len, page_plan, value_up):
    groups = lax.axis_size("dp")
    request_count, head_count, width = queries.shape
    targets = page_plan.reshape(groups)
    matched = targets[:, None] == lax.broadcasted_iota(jnp.int32, (groups, request_count), 1)
    onehot_table = matched.astype(jnp.bfloat16)
    outgoing = jnp.dot(
        onehot_table,
        queries.reshape(request_count, head_count * width),
        preferred_element_type=jnp.float32,
    )
    outgoing = outgoing.astype(jnp.bfloat16).reshape(groups, head_count, width)
    slot_cache = host_cache.reshape(groups, host_cache.shape[3], width)
    slot_lengths = host_len.reshape(groups)
    helper_out, helper_lse = attend(
        lax.all_to_all(outgoing, "dp", split_axis=0, concat_axis=0, tiled=True),
        slot_cache,
        slot_lengths,
    )
    back_out = lax.all_to_all(helper_out, "dp", split_axis=0, concat_axis=0, tiled=True)
    back_lse = lax.all_to_all(helper_lse, "dp", split_axis=0, concat_axis=0, tiled=True)
    own_out, own_lse = attend(queries, own_cache, own_len.reshape(request_count))
    masked = jnp.where(matched[:, :, None], back_lse[:, None, :], masked_score)
    largest = jnp.maximum(own_lse, jnp.max(masked, axis=0))
    own_weight = jnp.exp(own_lse - largest)
    help_weight = jnp.exp(masked - largest[None])
    gathered = jnp.einsum("pch,phd->chd", help_weight, back_out, precision=lax.Precision.HIGHEST)
    totals = own_weight + jnp.sum(help_weight, axis=0)
    device_out = (own_weight[..., None] * own_out + gathered) / totals[..., None]
    device_lse = largest + jnp.log(totals)
    latent, unused_lse = combine_group(device_out, device_lse)
    latent = latent.astype(jnp.bfloat16)
    result = jnp.einsum("chd,hde->che", latent, value_up, preferred_element_type=jnp.float32)
    return result.astype(jnp.bfloat16)


def solution(mesh):
    return jax.shard_map(
        local,
        mesh=mesh,
        in_specs=(
            P("dp", None, None),
            P("dp", "sub", None),
            P("dp", "sub"),
            P("dp", "sub", None, None, None),
            P("dp", "sub", None),
            P("dp", "sub", None),
            P("sub", None, None),
        ),
        out_specs=P("dp", "sub", None),
        check_vma=False,
    )
```

profile of v0, /device:TPU:0, one launch (start us, length us, event | category | flops | bytes accessed | tf_op | source)
XLA Modules:
  0.0 100.5 jit_solution(15990378591862014049)
XLA Ops:
  0.0 1.5 %reshape.178 = bf16[4,36864]{1,0:T(4,128)(2,1)S(1)} reshape(bf16[4,64,576]{2,1,0:T(8,128)(2,1)} %param.7) | data formatting | bytes 589824 | tf_op jit(solution)/shard_map/reshape | solution.py:49
  1.5 1.0 %convolution_convert_fusion = bf16[8,36864]{1,0:T(8,128)(2,1)S(1)} fusion(bf16[4,36864]{1,0:T(4,128)(2,1)S(1)} %reshape.178, s32[8]{0:T(128)} %bitcast.61), kind=kOutput, calls=%fused_computation | convolution fusion | flops 2654240 | bytes 884768 | tf_op jit(solution)/shard_map/dot_general | solution.py:47
  2.6 1.7 %reshape.179 = bf16[8,64,576]{2,1,0:T(8,128)(2,1)} reshape(bf16[8,36864]{1,0:T(8,128)(2,1)S(1)} %convolution_convert_fusion) | data formatting | bytes 1179648 | tf_op jit(solution)/shard_map/reshape | solution.py:52
  4.2 7.3 %all-to-all-start = ((bf16[8,64,576]{2,1,0:T(8,128)(2,1)}), bf16[8,64,576]{2,1,0:T(8,128)(2,1)S(1)}, u32[]{:S(2)}, u32[]{:S(2)}) async-start(bf16[8,64,576]{2,1,0:T(8,128)(2,1)} %reshape.179), calls=%async_computation | async-start | bytes 1310720 | tf_op jit(solution)/shard_map/all_to_all | solution.py:56
  11.5 14.1 %copy.28 = bf16[1,1,8,1024,576]{4,3,2,1,0:T(8,128)(2,1)} copy(bf16[1,1,8,1024,576]{3,4,2,1,0:T(8,128)(2,1)} %param.10) | data formatting | bytes 18874368 | tf_op args[3]
  25.7 3.1 %all-to-all-done = bf16[8,64,576]{2,1,0:T(8,128)(2,1)S(1)} async-done(((bf16[8,64,576]{2,1,0:T(8,128)(2,1)}), bf16[8,64,576]{2,1,0:T(8,128)(2,1)S(1)}, u32[]{:S(2)}, u32[]{:S(2)}) %all-to-all-start) | async-done | bytes 589856 | tf_op jit(solution)/shard_map/all_to_all | solution.py:56
  28.8 5.7 %fusion.4 = (f32[8,64]{1,0:T(8,128)S(1)}, f32[8,64,1024]{2,1,0:T(8,128)S(1)}) fusion(pred[8,1024]{1,0:T(8,128)(4,1)S(1)} %iota_compare_fusion, bf16[8,64,576]{2,1,0:T(8,128)(2,1)S(1)} %all-to-all-done, bf16[1,1,8,1024,576]{3,4,2,1,0:T(8,128)(2,1)} %param.10), kind=kOutput, calls=%fused_computation.7 | convolution fusion | flops 605552128 | bytes 12134400 | tf_op jit(solution)/shard_map/phd,ptd->pht/dot_general | solution.py:13
  34.5 1.3 %copy-done.1 = f32[8,64,1024]{2,1,0:T(8,128)} copy-done((f32[8,64,1024]{2,1,0:T(8,128)}, f32[8,64,1024]{2,1,0:T(8,128)S(1)}, u32[]{:S(2)}) %copy-start.1) | copy-done | bytes 2097176
  35.8 0.6 fusion.6
  36.4 0.6 log_add_fusion
  37.0 3.6 %all-to-all-start.1 = ((f32[8,1,64]{2,1,0:T(1,128)}), f32[8,1,64]{2,1,0:T(1,128)S(1)}, u32[]{:S(2)}, u32[]{:S(2)}) async-start(f32[8,1,64]{2,1,0:T(1,128)} %bitcast.6), calls=%async_computation.1 | async-start | bytes 8192 | tf_op jit(solution)/shard_map/all_to_all | solution.py:61
  40.6 6.7 %fusion.21 = f32[8,64,512]{2,1,0:T(8,128)} fusion(bf16[8,1024,576]{2,1,0:T(8,128)(2,1)} %bitcast.57, f32[8,64,1024]{2,1,0:T(8,128)} %copy-done.1, f32[8,64]{1,0:T(8,128)S(1)} %get-tuple-element.9, pred[8,1024]{1,0:T(8,128)(4,1)S(1)} %iota_compare_fusion, f32[8,64]{1,0:T(8,128)S(1)} %fusion.6), kind=kOutput, calls=%fused_computation.26 | convolution fusion | flops 539230208 | bytes 11546624 | tf_op jit(solution)/shard_map/pht,ptd->phd/dot_general | solution.py:22
  47.3 6.1 %all-to-all-start.3 = ((f32[8,64,512]{2,1,0:T(8,128)}), f32[8,64,512]{2,1,0:T(8,128)S(1)}, u32[]{:S(2)}, u32[]{:S(2)}) async-start(f32[8,64,512]{2,1,0:T(8,128)} %fusion.21), calls=%async_computation.3 | async-start | bytes 2097152 | tf_op jit(solution)/shard_map/all_to_all | solution.py:60
  53.5 1.7 %fusion.50 = (f32[4,64]{1,0:T(4,128)S(1)}, f32[4,64,256]{2,1,0:T(8,128)S(1)}) fusion(bf16[4,64,576]{2,1,0:T(8,128)(2,1)S(1)} %copy-done.2, bf16[4,256,576]{1,2,0:T(8,128)(2,1)} %param.8, pred[4,256]{1,0:T(4,128)(4,1)S(1)} %iota_compare_fusion.1), kind=kOutput, calls=%fused_computation.64 | convolution fusion | flops 75693824 | bytes 1738752 | tf_op jit(solution)/shard_map/phd,ptd->pht/dot_general | solution.py:13
  55.3 0.7 copy-done.3
  56.9 0.7 copy.35
  57.6 21.4 %all-to-all-done.3 = f32[8,64,512]{2,1,0:T(8,128)S(1)} async-done(((f32[8,64,512]{2,1,0:T(8,128)}), f32[8,64,512]{2,1,0:T(8,128)S(1)}, u32[]{:S(2)}, u32[]{:S(2)}) %all-to-all-start.3) | async-done | bytes 1048608 | tf_op jit(solution)/shard_map/all_to_all | solution.py:60
  79.0 3.3 %all-to-all-start.2 = ((f32[1,4,64]{1,0,2:T(1,128)}), f32[1,4,64]{1,0,2:T(1,128)S(1)}, u32[]{:S(2)}, u32[]{:S(2)}) async-start(f32[1,4,64]{1,0,2:T(1,128)} %copy.35), calls=%async_computation.2 | async-start | bytes 65536 | tf_op jit(solution)/shard_map/all_to_all | solution.py:31
  82.3 1.6 %fusion.14 = f32[64,512,4]{1,2,0:T(4,128)S(1)} fusion(f32[8,64,512]{2,1,0:T(8,128)S(1)} %all-to-all-done.3, f32[4,64]{0,1:T(8,128)S(1)} %copy.33, f32[8,64]{0,1:T(8,128)S(1)} %copy.30, pred[8,4]{0,1:T(4,128)(4,1)S(1)} %iota_compare_fusion.2), kind=kOutput, calls=%fused_computation.19 | convolution fusion | flops 12587008 | bytes 1575968 | tf_op jit(solution)/shard_map/pch,phd->chd/dot_general | solution.py:67
  83.9 1.8 %fusion.10 = f32[1,4,64,512]{3,2,1,0:T(8,128)S(1)} fusion(bf16[4,256,576]{1,2,0:T(8,128)(2,1)} %param.8, f32[64,512,4]{1,2,0:T(4,128)S(1)} %fusion.14, f32[4,64]{1,0:T(4,128)S(1)} %get-tuple-element.7, f32[4,64]{1,0:T(4,128)S(1)} %fusion.28, f32[4,64]{1,0:T(4,128)S(1)} %get-tuple-element.8, f32[4,64,256]{2,1,0:T(8,128)} %copy-done.3, ...), kind=kOutput, calls=%fused_computation.14 | convolution fusion | flops 67764224 | bytes 2363392 | tf_op jit(solution)/shard_map/pht,ptd->phd/dot_general | solution.py:22
  85.8 1.1 %copy.41 = f32[1,4,64,512]{3,1,0,2:T(4,128)} copy(f32[1,4,64,512]{3,2,1,0:T(8,128)S(1)} %fusion.10) | data formatting | bytes 1048576 | tf_op jit(solution)/shard_map/broadcast_in_dim | solution.py:30
  86.9 3.5 %all-to-all-start.4 = ((f32[1,4,64,512]{3,1,0,2:T(4,128)}), f32[1,4,64,512]{3,1,0,2:T(4,128)S(1)}, u32[]{:S(2)}, u32[]{:S(2)}) async-start(f32[1,4,64,512]{3,1,0,2:T(4,128)} %copy.41), calls=%async_computation.4 | async-start | bytes 1048576 | tf_op jit(solution)/shard_map/all_to_all | solution.py:30
  90.5 8.6 %all-to-all-done.4 = f32[1,4,64,512]{3,1,0,2:T(4,128)S(1)} async-done(((f32[1,4,64,512]{3,1,0,2:T(4,128)}), f32[1,4,64,512]{3,1,0,2:T(4,128)S(1)}, u32[]{:S(2)}, u32[]{:S(2)}) %all-to-all-start.4) | async-done | bytes 524320 | tf_op jit(solution)/shard_map/all_to_all | solution.py:30
  99.8 0.6 copy.44
  (33 shorter events, 1.9 us)
Async XLA Ops:
  0.0 99.4 %copy-start = (bf16[16,512,128]{2,1,0:T(8,128)(2,1)S(1)}, bf16[16,512,128]{2,1,0:T(8,128)(2,1)}, u32[]{:S(2)}) copy-start(bf16[16,512,128]{2,1,0:T(8,128)(2,1)} %param.13) | copy-start | bytes 6291460
  4.2 24.6 %all-to-all-start = ((bf16[8,64,576]{2,1,0:T(8,128)(2,1)}), bf16[8,64,576]{2,1,0:T(8,128)(2,1)S(1)}, u32[]{:S(2)}, u32[]{:S(2)}) async-start(bf16[8,64,576]{2,1,0:T(8,128)(2,1)} %reshape.179), calls=%async_computation | async-start | bytes 1310720 | tf_op jit(solution)/shard_map/all_to_all | solution.py:56
  11.5 14.1 %copy-start.5 = (s32[1,1,8]{2,1,0:T(1,128)S(1)}, s32[1,1,8]{2,1,0:T(1,128)}, u32[]{:S(2)}) copy-start(s32[1,1,8]{2,1,0:T(1,128)} %param.11) | copy-start | bytes 100
  34.5 1.3 %copy-start.1 = (f32[8,64,1024]{2,1,0:T(8,128)}, f32[8,64,1024]{2,1,0:T(8,128)S(1)}, u32[]{:S(2)}) copy-start(f32[8,64,1024]{2,1,0:T(8,128)S(1)} %get-tuple-element.10) | copy-start | bytes 6291460
  37.0 10.3 %all-to-all-start.1 = ((f32[8,1,64]{2,1,0:T(1,128)}), f32[8,1,64]{2,1,0:T(1,128)S(1)}, u32[]{:S(2)}, u32[]{:S(2)}) async-start(f32[8,1,64]{2,1,0:T(1,128)} %bitcast.6), calls=%async_computation.1 | async-start | bytes 8192 | tf_op jit(solution)/shard_map/all_to_all | solution.py:61
  47.3 6.1 %copy-start.6 = (s32[4,1]{0,1:T(1,128)S(1)}, s32[4,1]{0,1:T(1,128)}, u32[]{:S(2)}) copy-start(s32[4,1]{0,1:T(1,128)} %param.9) | copy-start | bytes 52
  47.3 6.2 %copy-start.2 = (bf16[4,64,576]{2,1,0:T(8,128)(2,1)S(1)}, bf16[4,64,576]{2,1,0:T(8,128)(2,1)}, u32[]{:S(2)}) copy-start(bf16[4,64,576]{2,1,0:T(8,128)(2,1)} %param.7) | copy-start | bytes 884740
  47.3 8.8 %copy-start.4 = (s32[1,1,8]{2,1,0:T(1,128)S(1)}, s32[1,1,8]{2,1,0:T(1,128)}, u32[]{:S(2)}) copy-start(s32[1,1,8]{2,1,0:T(1,128)} %param.12) | copy-start | bytes 100
  47.3 31.7 %all-to-all-start.3 = ((f32[8,64,512]{2,1,0:T(8,128)}), f32[8,64,512]{2,1,0:T(8,128)S(1)}, u32[]{:S(2)}, u32[]{:S(2)}) async-start(f32[8,64,512]{2,1,0:T(8,128)} %fusion.21), calls=%async_computation.3 | async-start | bytes 2097152 | tf_op jit(solution)/shard_map/all_to_all | solution.py:60
  55.3 0.7 copy-start.3
  79.0 7.9 %all-to-all-start.2 = ((f32[1,4,64]{1,0,2:T(1,128)}), f32[1,4,64]{1,0,2:T(1,128)S(1)}, u32[]{:S(2)}, u32[]{:S(2)}) async-start(f32[1,4,64]{1,0,2:T(1,128)} %copy.35), calls=%async_computation.2 | async-start | bytes 65536 | tf_op jit(solution)/shard_map/all_to_all | solution.py:31
  86.9 12.3 %all-to-all-start.4 = ((f32[1,4,64,512]{3,1,0,2:T(4,128)}), f32[1,4,64,512]{3,1,0,2:T(4,128)S(1)}, u32[]{:S(2)}, u32[]{:S(2)}) async-start(f32[1,4,64,512]{3,1,0,2:T(4,128)} %copy.41), calls=%async_computation.4 | async-start | bytes 1048576 | tf_op jit(solution)/shard_map/all_to_all | solution.py:30
where the time goes:
time: 101 us; the launch traced here: 100 us
  waiting for transfers between devices  33.1 us (33%)
  starting transfers between devices  23.8 us (24%)
  local copies, waits for them, and re-layouts  22.2 us (22%)
  matrix products  18.9 us (19%)
  other arithmetic  2.27 us (2%)
    all_to_all x1, waiting for transfers between devices, local(): lax.all_to_all(helper_out, 'dp', split_axis=0, concat_axis=0, tiled=True)  21.4 us
    unnamed x15, local copies, waits for them, and re-layouts  16.1 us
    all_to_all x1, waiting for transfers between devices, combine_group(): lax.all_to_all(device_out[None], 'sub', split_axis=2, concat_axis=0, tile...  8.63 us
    dot_general x2, matrix products, attend(): jnp.einsum('pht,ptd->phd', weights, slot_cache[:, :, :DL], preferred_elem...  8.5 us
    dot_general x2, matrix products, attend(): jnp.einsum('phd,ptd->pht', queries, slot_cache, preferred_element_type=jn...  7.35 us
    all_to_all x1, starting transfers between devices, local(): lax.all_to_all(outgoing, 'dp', split_axis=0, concat_axis=0, tiled=True)  7.31 us
    all_to_all x1, starting transfers between devices, local(): lax.all_to_all(helper_out, 'dp', split_axis=0, concat_axis=0, tiled=True)  6.13 us
    all_to_all x1, starting transfers between devices, local(): lax.all_to_all(helper_lse, 'dp', split_axis=0, concat_axis=0, tiled=True)  3.64 us
  transfers between devices with their start and end apart: 5, of which 3 were waited for; matrix products, arithmetic and copies ran while one was open for 29% of the time, Pallas kernels for 0%

commit v1 on v0

--- a/solution.py
+++ b/solution.py
@@ -6,6 +6,17 @@
 DL = 512
 score_scale = 192 ** (-0.5)
 masked_score = -1e30
+
+
+def split_up(x, dim, length):
+    before, after = (x.shape[:dim], x.shape[dim + 1 :])
+    return jnp.moveaxis(x.reshape(*before, length, -1, *after), dim, 0)
+
+
+def joined_along(blocks, dim):
+    shape = list(blocks.shape[1:])
+    shape[dim] *= blocks.shape[0]
+    return jnp.moveaxis(blocks, 0, dim).reshape(shape)
 
 
 def attend(queries, slot_cache, lengths):
@@ -58,7 +69,14 @@
         slot_lengths,
     )
     back_out = lax.all_to_all(helper_out, "dp", split_axis=0, concat_axis=0, tiled=True)
-    back_lse = lax.all_to_all(helper_lse, "dp", split_axis=0, concat_axis=0, tiled=True)
+    size, index = (lax.axis_size("dp"), lax.axis_index("dp"))
+    parts = split_up(helper_lse, 0, size)
+    outs = [parts[index]]
+    for turn in range(1, size):
+        sent = parts[index ^ turn]
+        outs.append(lax.ppermute(sent, "dp", [(i, i ^ turn) for i in range(size)]))
+    parts = jnp.stack(outs)[index ^ jnp.arange(size)]
+    back_lse = joined_along(parts, 0)
     own_out, own_lse = attend(queries, own_cache, own_len.reshape(request_count))
     masked = jnp.where(matched[:, :, None], back_lse[:, None, :], masked_score)
     largest = jnp.maximum(own_lse, jnp.max(masked, axis=0))

time: 101 us -> 93 us (0.921)
  waiting for transfers between devices: 33.1 us -> 19.7 us
  starting transfers between devices: 23.8 us -> 33 us
  matrix products: 18.9 us -> 15.5 us
  local copies, waits for them, and re-layouts: 22.2 us -> 21 us
    all_to_all x1, waiting for transfers between devices: 21.4 us -> 0.01 us  [local(): lax.all_to_all(helper_out, 'dp', split_axis=0, concat_axis=0, tiled=True)]
    ppermute x0 -> x7, starting transfers between devices: none -> 15.2 us  [local(): outs.append(lax.ppermute(sent, 'dp', [(i, i ^ turn) for i in range(size)]))]
    ppermute x0 -> x7, waiting for transfers between devices: none -> 8.05 us  [local(): outs.append(lax.ppermute(sent, 'dp', [(i, i ^ turn) for i in range(size)]))]
    dot_general x2, matrix products: 8.5 us -> 4.27 us  [attend(): jnp.einsum('pht,ptd->phd', weights, slot_cache[:, :, :DL], preferred_elem...]
    all_to_all x1 -> x0, starting transfers between devices: 3.64 us -> none  [local(): lax.all_to_all(helper_lse, 'dp', split_axis=0, concat_axis=0, tiled=True)]
    all_to_all x1, starting transfers between devices: 6.13 us -> 3.77 us  [local(): lax.all_to_all(helper_out, 'dp', split_axis=0, concat_axis=0, tiled=True)]
    unnamed x15, local copies, waits for them, and re-layouts: 16.1 us -> 14.3 us
    reduce_sum x2, other arithmetic: 0.78 us -> 1.82 us  [attend(): totals = jnp.sum(exponent, axis=2)]
  transfers between devices with their start and end apart: 5 -> 11, of which waited for: 3 -> 5; matrix products, arithmetic and copies ran while one was open for 29% -> 27% of each run, Pallas kernels for 0% -> 0%
where the time goes in v1:
time: 93 us; the launch traced here: 92.1 us
  starting transfers between devices  33 us (35%)
  local copies, waits for them, and re-layouts  21 us (23%)
  waiting for transfers between devices  19.7 us (21%)
  matrix products  15.5 us (17%)
  other arithmetic  2.72 us (3%)
    ppermute x7, starting transfers between devices, local(): outs.append(lax.ppermute(sent, 'dp', [(i, i ^ turn) for i in range(size)]))  15.2 us
    unnamed x15, local copies, waits for them, and re-layouts  14.3 us
    all_to_all x1, waiting for transfers between devices, combine_group(): lax.all_to_all(device_out[None], 'sub', split_axis=2, concat_axis=0, tile...  8.63 us
    dot_general x2, matrix products, attend(): jnp.einsum('phd,ptd->pht', queries, slot_cache, preferred_element_type=jn...  8.13 us
    ppermute x7, waiting for transfers between devices, local(): outs.append(lax.ppermute(sent, 'dp', [(i, i ^ turn) for i in range(size)]))  8.05 us
    all_to_all x1, starting transfers between devices, local(): lax.all_to_all(outgoing, 'dp', split_axis=0, concat_axis=0, tiled=True)  7.31 us
    dot_general x2, matrix products, attend(): jnp.einsum('pht,ptd->phd', weights, slot_cache[:, :, :DL], preferred_elem...  4.27 us
    all_to_all x1, starting transfers between devices, local(): lax.all_to_all(helper_out, 'dp', split_axis=0, concat_axis=0, tiled=True)  3.77 us
  transfers between devices with their start and end apart: 11, of which 5 were waited for; matrix products, arithmetic and copies ran while one was open for 27% of the time, Pallas kernels for 0%

profile of v1, /device:TPU:0, one launch (start us, length us, event | category | flops | bytes accessed | tf_op | source)
XLA Modules:
  0.0 92.1 jit_solution(2957919704929497258)
XLA Ops:
  0.0 1.5 %reshape.190 = bf16[4,36864]{1,0:T(4,128)(2,1)S(1)} reshape(bf16[4,64,576]{2,1,0:T(8,128)(2,1)} %param.7) | data formatting | bytes 589824 | tf_op jit(solution)/shard_map/reshape | solution.py:60
  2.6 1.7 %reshape.191 = bf16[8,64,576]{2,1,0:T(8,128)(2,1)} reshape(bf16[8,36864]{1,0:T(8,128)(2,1)S(1)} %convolution_convert_fusion) | data formatting | bytes 1179648 | tf_op jit(solution)/shard_map/reshape | solution.py:63
  4.2 7.3 %all-to-all-start = ((bf16[8,64,576]{2,1,0:T(8,128)(2,1)}), bf16[8,64,576]{2,1,0:T(8,128)(2,1)S(1)}, u32[]{:S(2)}, u32[]{:S(2)}) async-start(bf16[8,64,576]{2,1,0:T(8,128)(2,1)} %reshape.191), calls=%async_computation | async-start | bytes 1310720 | tf_op jit(solution)/shard_map/all_to_all | solution.py:67
  11.5 14.1 %copy.44 = bf16[1,1,8,1024,576]{4,3,2,1,0:T(8,128)(2,1)} copy(bf16[1,1,8,1024,576]{3,4,2,1,0:T(8,128)(2,1)} %param.10) | data formatting | bytes 18874368 | tf_op args[3]
  25.8 3.0 %all-to-all-done = bf16[8,64,576]{2,1,0:T(8,128)(2,1)S(1)} async-done(((bf16[8,64,576]{2,1,0:T(8,128)(2,1)}), bf16[8,64,576]{2,1,0:T(8,128)(2,1)S(1)}, u32[]{:S(2)}, u32[]{:S(2)}) %all-to-all-start) | async-done | bytes 589856 | tf_op jit(solution)/shard_map/all_to_all | solution.py:67
  28.8 5.8 %fusion.4 = (f32[8,64]{1,0:T(8,128)S(1)}, f32[8,64,1024]{2,1,0:T(8,128)S(1)}) fusion(pred[8,1024]{1,0:T(8,128)(4,1)S(1)} %iota_compare_fusion, bf16[8,64,576]{2,1,0:T(8,128)(2,1)S(1)} %all-to-all-done, bf16[1,1,8,1024,576]{3,4,2,1,0:T(8,128)(2,1)} %param.10), kind=kOutput, calls=%fused_computation.8 | convolution fusion | flops 605552128 | bytes 12134400 | tf_op jit(solution)/shard_map/phd,ptd->pht/dot_general | solution.py:24
  35.5 2.5 %fusion.21 = f32[8,64,512]{2,1,0:T(8,128)} fusion(bf16[8,1024,576]{2,1,0:T(8,128)(2,1)S(1)} %bitcast.83, f32[8,64,1024]{2,1,0:T(8,128)S(1)} %get-tuple-element.18, f32[8,64]{1,0:T(8,128)S(1)} %get-tuple-element.17, pred[8,1024]{1,0:T(8,128)(4,1)S(1)} %iota_compare_fusion, f32[8,64]{1,0:T(8,128)S(1)} %fusion.6), kind=kOutput, calls=%fused_computation.27 | convolution fusion | flops 539230208 | bytes 11550720 | tf_op jit(solution)/shard_map/pht,ptd->phd/dot_general | solution.py:33
  38.0 3.8 %all-to-all-start.2 = ((f32[8,64,512]{2,1,0:T(8,128)}), f32[8,64,512]{2,1,0:T(8,128)S(1)}, u32[]{:S(2)}, u32[]{:S(2)}) async-start(f32[8,64,512]{2,1,0:T(8,128)} %fusion.21), calls=%async_computation.2 | async-start | bytes 2097152 | tf_op jit(solution)/shard_map/all_to_all | solution.py:71
  41.8 2.3 %fusion.52 = (f32[4,64]{1,0:T(4,128)S(1)}, f32[4,64,256]{2,1,0:T(8,128)}) fusion(bf16[4,64,576]{2,1,0:T(8,128)(2,1)S(1)} %copy-done.2, bf16[4,256,576]{1,2,0:T(8,128)(2,1)} %param.8, pred[4,256]{1,0:T(4,128)(4,1)S(1)} %iota_compare_fusion.1), kind=kOutput, calls=%fused_computation.77 | convolution fusion | flops 75693824 | bytes 1738752 | tf_op jit(solution)/shard_map/phd,ptd->pht/dot_general | solution.py:24
  44.2 1.2 %fusion.28 = f32[4,64]{1,0:T(4,128)S(1)} fusion(f32[4,64,256]{2,1,0:T(8,128)} %get-tuple-element.20, f32[4,64]{1,0:T(4,128)S(1)} %get-tuple-element.19), kind=kLoop, calls=%fused_computation.32 | loop fusion | flops 130816 | bytes 264192 | tf_op jit(solution)/shard_map/reduce_sum | solution.py:31
  45.4 2.1 %collective-permute-start = (f32[1,64]{1,0:T(1,128)S(1)}, f32[1,64]{1,0:T(1,128)S(1)}, u32[]{:S(2)}, u32[]{:S(2)}) collective-permute-start(f32[1,64]{1,0:T(1,128)S(1)} %get-tuple-element.15), channel_id=1, source_target_pairs={{0,4},{4,0},{8,12},{12,8},{16,20},{20,16},{24,28},{28,24},{1,5},{5... | collective-permute-start | bytes 776 | tf_op jit(solution)/shard_map/ppermute | solution.py:77
  47.5 1.5 %collective-permute-start.1 = (f32[1,64]{1,0:T(1,128)S(1)}, f32[1,64]{1,0:T(1,128)S(1)}, u32[]{:S(2)}, u32[]{:S(2)}) collective-permute-start(f32[1,64]{1,0:T(1,128)S(1)} %get-tuple-element.14), channel_id=1, source_target_pairs={{0,8},{4,12},{8,0},{12,4},{16,24},{20,28},{24,16},{28,20},{1,9},{5... | collective-permute-start | bytes 776 | tf_op jit(solution)/shard_map/ppermute | solution.py:77
  49.1 2.8 %collective-permute-start.3 = (f32[1,64]{1,0:T(1,128)S(1)}, f32[1,64]{1,0:T(1,128)S(1)}, u32[]{:S(2)}, u32[]{:S(2)}) collective-permute-start(f32[1,64]{1,0:T(1,128)S(1)} %get-tuple-element.12), channel_id=1, source_target_pairs={{0,16},{4,20},{8,24},{12,28},{16,0},{20,4},{24,8},{28,12},{1,17},{... | collective-permute-start | bytes 776 | tf_op jit(solution)/shard_map/ppermute | solution.py:77
  51.9 1.5 %collective-permute-start.4 = (f32[1,64]{1,0:T(1,128)S(1)}, f32[1,64]{1,0:T(1,128)S(1)}, u32[]{:S(2)}, u32[]{:S(2)}) collective-permute-start(f32[1,64]{1,0:T(1,128)S(1)} %get-tuple-element.11), channel_id=1, source_target_pairs={{0,20},{4,16},{8,28},{12,24},{16,4},{20,0},{24,12},{28,8},{1,21},{... | collective-permute-start | bytes 776 | tf_op jit(solution)/shard_map/ppermute | solution.py:77
  53.4 3.3 %collective-permute-start.5 = (f32[1,64]{1,0:T(1,128)S(1)}, f32[1,64]{1,0:T(1,128)S(1)}, u32[]{:S(2)}, u32[]{:S(2)}) collective-permute-start(f32[1,64]{1,0:T(1,128)S(1)} %get-tuple-element.10), channel_id=1, source_target_pairs={{0,24},{4,28},{8,16},{12,20},{16,8},{20,12},{24,0},{28,4},{1,25},{... | collective-permute-start | bytes 776 | tf_op jit(solution)/shard_map/ppermute | solution.py:77
  56.6 3.0 %collective-permute-done.1 = f32[1,64]{1,0:T(1,128)S(1)} collective-permute-done((f32[1,64]{1,0:T(1,128)S(1)}, f32[1,64]{1,0:T(1,128)S(1)}, u32[]{:S(2)}, u32[]{:S(2)}) %collective-permute-start.1) | collective-permute-done | bytes 288 | tf_op jit(solution)/shard_map/ppermute | solution.py:77
  59.6 4.0 %collective-permute-start.6 = (f32[1,64]{1,0:T(1,128)S(1)}, f32[1,64]{1,0:T(1,128)S(1)}, u32[]{:S(2)}, u32[]{:S(2)}) collective-permute-start(f32[1,64]{1,0:T(1,128)S(1)} %get-tuple-element.9), channel_id=1, source_target_pairs={{0,28},{4,24},{8,20},{12,16},{16,12},{20,8},{24,4},{28,0},{1,29},{... | collective-permute-start | bytes 776 | tf_op jit(solution)/shard_map/ppermute | solution.py:77
  63.6 4.3 %collective-permute-done.3 = f32[1,64]{1,0:T(1,128)S(1)} collective-permute-done((f32[1,64]{1,0:T(1,128)S(1)}, f32[1,64]{1,0:T(1,128)S(1)}, u32[]{:S(2)}, u32[]{:S(2)}) %collective-permute-start.3) | collective-permute-done | bytes 288 | tf_op jit(solution)/shard_map/ppermute | solution.py:77
  70.8 3.3 %all-to-all-start.1 = ((f32[1,4,64]{1,0,2:T(1,128)}), f32[1,4,64]{1,0,2:T(1,128)S(1)}, u32[]{:S(2)}, u32[]{:S(2)}) async-start(f32[1,4,64]{1,0,2:T(1,128)} %copy.59), calls=%async_computation.1 | async-start | bytes 65536 | tf_op jit(solution)/shard_map/all_to_all | solution.py:42
  74.1 1.6 %fusion.14 = f32[64,512,4]{1,2,0:T(4,128)S(1)} fusion(f32[8,64,512]{2,1,0:T(8,128)S(1)} %all-to-all-done.2, f32[8,64]{0,1:T(8,128)S(1)} %copy.54, f32[4,64]{0,1:T(8,128)S(1)} %copy.57, pred[8,4]{0,1:T(4,128)(4,1)S(1)} %iota_compare_fusion.2), kind=kOutput, calls=%fused_computation.20 | convolution fusion | flops 12587008 | bytes 1575968 | tf_op jit(solution)/shard_map/pch,phd->chd/dot_general | solution.py:85
  75.7 1.7 %fusion.10 = f32[1,4,64,512]{3,2,1,0:T(8,128)S(1)} fusion(bf16[4,256,576]{1,2,0:T(8,128)(2,1)} %param.8, f32[64,512,4]{1,2,0:T(4,128)S(1)} %fusion.14, f32[4,64]{1,0:T(4,128)S(1)} %get-tuple-element.7, f32[4,64]{1,0:T(4,128)S(1)} %fusion.28, f32[4,64]{1,0:T(4,128)S(1)} %get-tuple-element.8, f32[4,64,256]{2,1,0:T(8,128)S(1)} %copy-done.3, ...), kind=kOutput, calls=%fused_computation.15 | convolution fusion | flops 67764224 | bytes 2363392 | tf_op jit(solution)/shard_map/pht,ptd->phd/dot_general | solution.py:33
  77.5 1.1 %copy.65 = f32[1,4,64,512]{3,1,0,2:T(4,128)} copy(f32[1,4,64,512]{3,2,1,0:T(8,128)S(1)} %fusion.10) | data formatting | bytes 1048576 | tf_op jit(solution)/shard_map/broadcast_in_dim | solution.py:41
  78.6 3.5 %all-to-all-start.3 = ((f32[1,4,64,512]{3,1,0,2:T(4,128)}), f32[1,4,64,512]{3,1,0,2:T(4,128)S(1)}, u32[]{:S(2)}, u32[]{:S(2)}) async-start(f32[1,4,64,512]{3,1,0,2:T(4,128)} %copy.65), calls=%async_computation.3 | async-start | bytes 1048576 | tf_op jit(solution)/shard_map/all_to_all | solution.py:41
  82.2 8.6 %all-to-all-done.3 = f32[1,4,64,512]{3,1,0,2:T(4,128)S(1)} async-done(((f32[1,4,64,512]{3,1,0,2:T(4,128)}), f32[1,4,64,512]{3,1,0,2:T(4,128)S(1)}, u32[]{:S(2)}, u32[]{:S(2)}) %all-to-all-start.3) | async-done | bytes 524320 | tf_op jit(solution)/shard_map/all_to_all | solution.py:41
  (50 shorter events, 6.4 us)
Async XLA Ops:
  0.0 91.1 %copy-start = (bf16[16,512,128]{2,1,0:T(8,128)(2,1)S(1)}, bf16[16,512,128]{2,1,0:T(8,128)(2,1)}, u32[]{:S(2)}) copy-start(bf16[16,512,128]{2,1,0:T(8,128)(2,1)} %param.13) | copy-start | bytes 6291460
  4.2 24.6 %all-to-all-start = ((bf16[8,64,576]{2,1,0:T(8,128)(2,1)}), bf16[8,64,576]{2,1,0:T(8,128)(2,1)S(1)}, u32[]{:S(2)}, u32[]{:S(2)}) async-start(bf16[8,64,576]{2,1,0:T(8,128)(2,1)} %reshape.191), calls=%async_computation | async-start | bytes 1310720 | tf_op jit(solution)/shard_map/all_to_all | solution.py:67
  11.5 14.1 %copy-start.6 = (s32[4,1]{0,1:T(1,128)S(1)}, s32[4,1]{0,1:T(1,128)}, u32[]{:S(2)}) copy-start(s32[4,1]{0,1:T(1,128)} %param.9) | copy-start | bytes 52
  11.5 14.2 %copy-start.5 = (s32[1,1,8]{2,1,0:T(1,128)S(1)}, s32[1,1,8]{2,1,0:T(1,128)}, u32[]{:S(2)}) copy-start(s32[1,1,8]{2,1,0:T(1,128)} %param.11) | copy-start | bytes 100
  28.8 6.7 %copy-start.1 = (bf16[1,1,8,1024,576]{4,3,2,1,0:T(8,128)(2,1)S(1)}, bf16[1,1,8,1024,576]{4,3,2,1,0:T(8,128)(2,1)}, u32[]{:S(2)}) copy-start(bf16[1,1,8,1024,576]{4,3,2,1,0:T(8,128)(2,1)} %copy.44) | copy-start | bytes 28311556
  38.0 3.8 %copy-start.2 = (bf16[4,64,576]{2,1,0:T(8,128)(2,1)S(1)}, bf16[4,64,576]{2,1,0:T(8,128)(2,1)}, u32[]{:S(2)}) copy-start(bf16[4,64,576]{2,1,0:T(8,128)(2,1)} %param.7) | copy-start | bytes 884740
  38.0 7.3 %copy-start.4 = (s32[1,1,8]{2,1,0:T(1,128)S(1)}, s32[1,1,8]{2,1,0:T(1,128)}, u32[]{:S(2)}) copy-start(s32[1,1,8]{2,1,0:T(1,128)} %param.12) | copy-start | bytes 100
  38.0 32.7 %all-to-all-start.2 = ((f32[8,64,512]{2,1,0:T(8,128)}), f32[8,64,512]{2,1,0:T(8,128)S(1)}, u32[]{:S(2)}, u32[]{:S(2)}) async-start(f32[8,64,512]{2,1,0:T(8,128)} %fusion.21), calls=%async_computation.2 | async-start | bytes 2097152 | tf_op jit(solution)/shard_map/all_to_all | solution.py:71
  44.2 31.6 %copy-start.3 = (f32[4,64,256]{2,1,0:T(8,128)S(1)}, f32[4,64,256]{2,1,0:T(8,128)}, u32[]{:S(2)}) copy-start(f32[4,64,256]{2,1,0:T(8,128)} %get-tuple-element.20) | copy-start | bytes 786436
  45.4 7.9 %collective-permute-start = (f32[1,64]{1,0:T(1,128)S(1)}, f32[1,64]{1,0:T(1,128)S(1)}, u32[]{:S(2)}, u32[]{:S(2)}) collective-permute-start(f32[1,64]{1,0:T(1,128)S(1)} %get-tuple-element.15), channel_id=1, source_target_pairs={{0,4},{4,0},{8,12},{12,8},{16,20},{20,16},{24,28},{28,24},{1,5},{5... | collective-permute-start | bytes 776 | tf_op jit(solution)/shard_map/ppermute | solution.py:77
  47.5 12.1 %collective-permute-start.1 = (f32[1,64]{1,0:T(1,128)S(1)}, f32[1,64]{1,0:T(1,128)S(1)}, u32[]{:S(2)}, u32[]{:S(2)}) collective-permute-start(f32[1,64]{1,0:T(1,128)S(1)} %get-tuple-element.14), channel_id=1, source_target_pairs={{0,8},{4,12},{8,0},{12,4},{16,24},{20,28},{24,16},{28,20},{1,9},{5... | collective-permute-start | bytes 776 | tf_op jit(solution)/shard_map/ppermute | solution.py:77
  49.0 14.7 %collective-permute-start.2 = (f32[1,64]{1,0:T(1,128)S(1)}, f32[1,64]{1,0:T(1,128)S(1)}, u32[]{:S(2)}, u32[]{:S(2)}) collective-permute-start(f32[1,64]{1,0:T(1,128)S(1)} %get-tuple-element.13), channel_id=1, source_target_pairs={{0,12},{4,8},{8,4},{12,0},{16,28},{20,24},{24,20},{28,16},{1,13},{... | collective-permute-start | bytes 776 | tf_op jit(solution)/shard_map/ppermute | solution.py:77
  49.1 18.9 %collective-permute-start.3 = (f32[1,64]{1,0:T(1,128)S(1)}, f32[1,64]{1,0:T(1,128)S(1)}, u32[]{:S(2)}, u32[]{:S(2)}) collective-permute-start(f32[1,64]{1,0:T(1,128)S(1)} %get-tuple-element.12), channel_id=1, source_target_pairs={{0,16},{4,20},{8,24},{12,28},{16,0},{20,4},{24,8},{28,12},{1,17},{... | collective-permute-start | bytes 776 | tf_op jit(solution)/shard_map/ppermute | solution.py:77
  51.9 16.8 %collective-permute-start.4 = (f32[1,64]{1,0:T(1,128)S(1)}, f32[1,64]{1,0:T(1,128)S(1)}, u32[]{:S(2)}, u32[]{:S(2)}) collective-permute-start(f32[1,64]{1,0:T(1,128)S(1)} %get-tuple-element.11), channel_id=1, source_target_pairs={{0,20},{4,16},{8,28},{12,24},{16,4},{20,0},{24,12},{28,8},{1,21},{... | collective-permute-start | bytes 776 | tf_op jit(solution)/shard_map/ppermute | solution.py:77
  53.4 15.3 %collective-permute-start.5 = (f32[1,64]{1,0:T(1,128)S(1)}, f32[1,64]{1,0:T(1,128)S(1)}, u32[]{:S(2)}, u32[]{:S(2)}) collective-permute-start(f32[1,64]{1,0:T(1,128)S(1)} %get-tuple-element.10), channel_id=1, source_target_pairs={{0,24},{4,28},{8,16},{12,20},{16,8},{20,12},{24,0},{28,4},{1,25},{... | collective-permute-start | bytes 776 | tf_op jit(solution)/shard_map/ppermute | solution.py:77
  59.6 9.1 %collective-permute-start.6 = (f32[1,64]{1,0:T(1,128)S(1)}, f32[1,64]{1,0:T(1,128)S(1)}, u32[]{:S(2)}, u32[]{:S(2)}) collective-permute-start(f32[1,64]{1,0:T(1,128)S(1)} %get-tuple-element.9), channel_id=1, source_target_pairs={{0,28},{4,24},{8,20},{12,16},{16,12},{20,8},{24,4},{28,0},{1,29},{... | collective-permute-start | bytes 776 | tf_op jit(solution)/shard_map/ppermute | solution.py:77
  70.8 7.8 %all-to-all-start.1 = ((f32[1,4,64]{1,0,2:T(1,128)}), f32[1,4,64]{1,0,2:T(1,128)S(1)}, u32[]{:S(2)}, u32[]{:S(2)}) async-start(f32[1,4,64]{1,0,2:T(1,128)} %copy.59), calls=%async_computation.1 | async-start | bytes 65536 | tf_op jit(solution)/shard_map/all_to_all | solution.py:42
  78.6 12.3 %all-to-all-start.3 = ((f32[1,4,64,512]{3,1,0,2:T(4,128)}), f32[1,4,64,512]{3,1,0,2:T(4,128)S(1)}, u32[]{:S(2)}, u32[]{:S(2)}) async-start(f32[1,4,64,512]{3,1,0,2:T(4,128)} %copy.65), calls=%async_computation.3 | async-start | bytes 1048576 | tf_op jit(solution)/shard_map/all_to_all | solution.py:41
